TPU v7x, 32 devices: a whole 2x2x4 slice. The times are simulated.
32 devices in a mesh: grp: 2 (over x), sp: 16 (over z, y, core).
Axes of the slice: x: 2, y: 2, z: 4, core: 2. Of those that a mesh axis runs over, the one named last changes fastest.
Arguments:
- field_in: bfloat16 [256, 16, 128, 512], P(('grp', 'sp')), parts along dimension 0, may hold values from -6 to 6
- out_grad: bfloat16 [256, 16, 128, 512], P(('grp', 'sp')), parts along dimension 0, may hold values from -6 to 6
- spectral_weight: bfloat16 [192, 96, 2, 256], P('sp'), may hold values from -6 to 6
- bypass_weight: bfloat16 [16, 16], replicated, may hold values from -1.5 to 1.5
- mode_x: int32 [12], replicated, may hold values from 0 to 127, as said below
- mode_y: int32 [16], replicated, may hold values from 0 to 127, as said below
- mode_z: int32 [12], replicated, may hold values from 0 to 31, as said below
- mode_t: int32 [8], replicated, may hold values from 0 to 15, as said below
Outputs:
- in_grad: bfloat16 [256, 16, 128, 512], P(('grp', 'sp')), parts along dimension 0
- weight_grad: float32 [384, 96, 2, 256], P(('grp', 'sp')), parts along dimension 0
- bypass_grad: float32 [32, 16], P('grp'), parts along dimension 0
There are 2 independent parts, one for each index of `grp`. A program takes and returns all parts, laid end to end along the dimension named above; an argument that names none is the same for every part. Nothing has to cross between parts.
Inputs may be any that keep to these rules, and one draw needn't show every extreme that they name: `mode_x`: 12 distinct frequencies, among them 0 and 127. `mode_y`: 16 distinct frequencies, among them 0 and 127. `mode_z`: 12 distinct frequencies, among them 0 and 31. `mode_t`: 8 distinct frequencies, among them 0 and 15.
All inputs are finite; a program needn't handle non-finite values.
Results may differ from a plain program's by a relative error of at most 0.0015.
Values sent between devices are 32-bit elements; how exact they have to be, the bound alone decides.
No kernel may reach another device: no remote copies, remote signals or barrier semaphores. Data moves between devices by JAX's collectives and lax.ppermute only.
A program may use at most 192 MiB of HBM per device.

v0:
```python
import math

import jax
import jax.numpy as jnp
from jax import lax
from jax.sharding import PartitionSpec as P

X = 128
Y = 128
Z = 32
STEPS = 16
C = 16
KX = 12
KY = 16
KZ = 12
KT = 8


HIGH = lax.Precision.HIGHEST


def block_table(frequencies, length):
    positions = jnp.arange(length, dtype=jnp.int32)
    phase_ints = positions[:, None] * frequencies[None, :] % length
    angles = 2.0 * math.pi / length * phase_ints.astype(jnp.float32)
    factor = 1.0 / math.sqrt(length)
    cosines = jnp.cos(angles) * factor
    sines = jnp.sin(angles) * factor
    real_in = jnp.stack([cosines, -sines], axis=-1)
    imag_in = jnp.stack([sines, cosines], axis=-1)
    return jnp.stack([real_in, imag_in], axis=1)


def plane_table(modes_depth, modes_time):
    depth_pos = jnp.arange(Z, dtype=jnp.int32)
    step_pos = jnp.arange(STEPS, dtype=jnp.int32)
    part_z = depth_pos[:, None] * modes_depth[None, :] % Z
    part_t = step_pos[:, None] * modes_time[None, :] % STEPS
    phase_ints = (part_z[:, None, :, None] * STEPS + part_t[None, :, None, :] * Z) % (Z * STEPS)
    angles = 2.0 * math.pi / (Z * STEPS) * phase_ints.astype(jnp.float32)
    factor = 1.0 / math.sqrt(Z * STEPS)
    table = jnp.stack([jnp.cos(angles), -jnp.sin(angles)], axis=2) * factor
    return table.reshape(Z * STEPS, 2 * KZ * KT)


def mixing(spec_u, spec_g, weights):
    modes_dev = spec_u.shape[0]
    wfull = weights.astype(jnp.float32).reshape(modes_dev, KX, KT, 2, C, C)
    w_re = wfull[:, :, :, 0]
    w_im = wfull[:, :, :, 1]
    u_re = spec_u[:, :, :, 0]
    u_im = spec_u[:, :, :, 1]
    g_re = spec_g[:, :, :, 0]
    g_im = spec_g[:, :, :, 1]
    adj_re = jnp.einsum("mktco,mkto->mktc", w_re, g_re, precision=HIGH) + jnp.einsum(
        "mktco,mkto->mktc", w_im, g_im, precision=HIGH
    )
    adj_im = jnp.einsum("mktco,mkto->mktc", w_re, g_im, precision=HIGH) - jnp.einsum(
        "mktco,mkto->mktc", w_im, g_re, precision=HIGH
    )
    grad_re = u_re[..., :, None] * g_re[..., None, :] + u_im[..., :, None] * g_im[..., None, :]
    grad_im = u_re[..., :, None] * g_im[..., None, :] - u_im[..., :, None] * g_re[..., None, :]
    adjoint = jnp.stack([adj_re, adj_im], axis=3)
    gradient = jnp.stack([grad_re, grad_im], axis=3).reshape(modes_dev, KX * KT, 2, C * C)
    return (adjoint, gradient)


def local_spectra(field, plane, ytab):
    slab_rows = field.shape[0]
    planes_zt = jnp.einsum(
        "xcyn,nm->xcym", field, plane, precision=HIGH, preferred_element_type=jnp.float32
    )
    planes_zt = planes_zt.reshape(slab_rows, C, Y, 2, KZ, KT)
    spectra = jnp.einsum("xcypzt,ypkq->xkzcqt", planes_zt, ytab, precision=HIGH)
    return spectra.reshape(slab_rows, KY * KZ, C * 2 * KT)


def shards(field_in, out_grad, spectral_weight, bypass_weight, mode_x, mode_y, mode_z, mode_t):
    slab_rows = field_in.shape[0]
    modes_dev = spectral_weight.shape[0]
    plane = plane_table(mode_z, mode_t)
    ytab = block_table(mode_y, Y)
    xtab = block_table(mode_x, X)
    local_u = local_spectra(field_in, plane, ytab)
    local_g = local_spectra(out_grad, plane, ytab)
    moved_u, moved_g = (
        lax.all_to_all(local_u, "sp", split_axis=1, concat_axis=0, tiled=True),
        lax.all_to_all(local_g, "sp", split_axis=1, concat_axis=0, tiled=True),
    )
    spec_u = jnp.einsum(
        "xmcpt,xpkq->mktqc", moved_u.reshape(X, modes_dev, C, 2, KT), xtab, precision=HIGH
    )
    spec_g = jnp.einsum(
        "xmcpt,xpkq->mktqc", moved_g.reshape(X, modes_dev, C, 2, KT), xtab, precision=HIGH
    )
    adjoint, weight_grad = mixing(spec_u, spec_g, spectral_weight)
    slabs = jnp.einsum("mktpc,xqkp->xmcqt", adjoint, xtab, precision=HIGH).reshape(
        X, modes_dev, C * 2 * KT
    )
    returned = lax.all_to_all(slabs, "sp", split_axis=0, concat_axis=1, tiled=True)
    back_rows = returned.reshape(slab_rows, KY, KZ, C, 2, KT)
    planes_zt = jnp.einsum("xkzcpt,yqkp->xcyqzt", back_rows, ytab, precision=HIGH).reshape(
        slab_rows, C, Y, 2 * KZ * KT
    )
    spectral = jnp.einsum("xcym,nm->xcyn", planes_zt, plane, precision=HIGH)
    bypass = jnp.einsum(
        "co,xoyn->xcyn", bypass_weight, out_grad, preferred_element_type=jnp.float32
    )
    in_grad = (spectral + bypass).astype(jnp.bfloat16)
    partial_total = jnp.einsum(
        "xcyn,xoyn->co", field_in, out_grad, preferred_element_type=jnp.float32
    )
    total = lax.psum(partial_total, "sp")
    bypass_grad = total / math.sqrt(X * Y * Z * STEPS)
    return (in_grad, weight_grad, bypass_grad)


def solution(mesh):
    return jax.shard_map(
        shards,
        mesh=mesh,
        in_specs=(
            P(("grp", "sp"), None, None, None),
            P(("grp", "sp"), None, None, None),
            P("sp", None, None, None),
            P(),
            P(),
            P(),
            P(),
            P(),
        ),
        out_specs=(
            P(("grp", "sp"), None, None, None),
            P(("grp", "sp"), None, None, None),
            P("grp", None),
        ),
        check_vma=False,
    )
```

profile of v0, /device:TPU:0, one launch (start us, length us, event | category | flops | bytes accessed | tf_op | source)
XLA Modules:
  0.0 664.5 jit_solution(10537567986778005111)
XLA Ops:
  3.5 6.2 fusion.46
  10.1 2.5 reshape.520
  12.6 30.0 %fusion.50 = f32[192,8,16,128]{3,0,2,1:T(8,128)S(1)} fusion(bf16[8,16,128,512]{3,2,1,0:T(8,128)(2,1)} %param.9, f32[512,192,1,1]{0,1,2,3:T(8,128)S(1)} %reshape.520), kind=kOutput, calls=%fused_computation.63 | convolution fusion | flops 19327352832 | bytes 29753344 | tf_op jit(solution)/shard_map/xcyn,nm->xcym/dot_general | solution.py:70
  42.7 54.1 %fusion.12 = f32[8,16,12,16,2,8]{3,1,5,2,0,4:T(8,128)} fusion(f32[8,16,128,2,12,8]{2,5,4,3,1,0:T(8,128)S(1)} %bitcast.198, f32[128,1,16,2]{0,2,1,3:T(8,128)S(1)} %get-tuple-element.25, f32[128,1,16,2]{0,2,1,3:T(8,128)S(1)} %get-tuple-element.24), kind=kOutput, calls=%fused_computation.17 | convolution fusion | flops 1207967744 | bytes 14188544 | tf_op jit(solution)/shard_map/xcypzt,ypkq->xkzcqt/dot_general | solution.py:74
  96.7 21.8 %copy.83 = f32[8,16,12,16,2,8]{2,1,5,4,3,0:T(8,128)} copy(f32[8,16,12,16,2,8]{3,1,5,2,0,4:T(8,128)} %fusion.12) | data formatting | bytes 3145728 | tf_op jit(solution)/shard_map/xcypzt,ypkq->xkzcqt/transpose | solution.py:74
  118.5 12.0 %reshape.511 = f32[8,192,256]{1,2,0:T(8,128)S(1)} reshape(f32[8,16,12,16,2,8]{2,1,5,4,3,0:T(8,128)} %copy.83) | data formatting | bytes 3145728 | tf_op jit(solution)/shard_map/reshape | solution.py:75
  130.6 1.7 copy.84
  132.3 7.5 %all-to-all-start = ((f32[8,192,256]{2,0,1:T(8,128)}), f32[8,192,256]{2,0,1:T(8,128)}, u32[]{:S(2)}, u32[]{:S(2)}) async-start(f32[8,192,256]{2,0,1:T(8,128)} %copy.84), calls=%async_computation | async-start | bytes 3145728 | tf_op jit(solution)/shard_map/all_to_all | solution.py:88
  139.8 20.8 %fusion.47 = f32[192,8,16,128]{3,0,2,1:T(8,128)} fusion(bf16[8,16,128,512]{3,2,1,0:T(8,128)(2,1)} %param.8, f32[512,192,1,1]{0,1,2,3:T(8,128)S(1)} %reshape.520), kind=kOutput, calls=%fused_computation.60 | convolution fusion | flops 19327352832 | bytes 29753344 | tf_op jit(solution)/shard_map/xcyn,nm->xcym/dot_general | solution.py:70
  160.6 23.4 %copy.106 = bf16[8,16,128,512]{2,1,0,3:T(8,128)(2,1)} copy(bf16[8,16,128,512]{3,2,1,0:T(8,128)(2,1)} %param.8) | data formatting | bytes 33554432 | tf_op args[0]
  184.0 23.4 %copy.107 = bf16[8,16,128,512]{2,1,0,3:T(8,128)(2,1)} copy(bf16[8,16,128,512]{3,2,1,0:T(8,128)(2,1)} %param.9) | data formatting | bytes 33554432 | tf_op args[1]
  207.3 55.0 %fusion.18 = f32[8,16,12,16,2,8]{3,1,5,2,0,4:T(8,128)} fusion(f32[8,16,128,2,12,8]{2,5,4,3,1,0:T(8,128)} %bitcast.199, f32[128,1,16,2]{0,2,1,3:T(8,128)S(1)} %get-tuple-element.25, f32[128,1,16,2]{0,2,1,3:T(8,128)S(1)} %get-tuple-element.24), kind=kOutput, calls=%fused_computation.19 | convolution fusion | flops 1207967744 | bytes 14188544 | tf_op jit(solution)/shard_map/xcypzt,ypkq->xkzcqt/dot_general | solution.py:74
  262.3 21.6 %copy.98 = f32[8,16,12,16,2,8]{2,1,5,4,3,0:T(8,128)} copy(f32[8,16,12,16,2,8]{3,1,5,2,0,4:T(8,128)} %fusion.18) | data formatting | bytes 3145728 | tf_op jit(solution)/shard_map/xcypzt,ypkq->xkzcqt/transpose | solution.py:74
  283.9 12.2 %reshape.518 = f32[8,192,256]{1,2,0:T(8,128)S(1)} reshape(f32[8,16,12,16,2,8]{2,1,5,4,3,0:T(8,128)} %copy.98) | data formatting | bytes 3145728 | tf_op jit(solution)/shard_map/reshape | solution.py:75
  296.1 1.8 copy.99
  297.9 14.1 %convolution_bitcast_fusion = f32[16,16]{1,0:T(8,128)S(1)} fusion(bf16[8,16,128,512]{2,1,0,3:T(8,128)(2,1)} %copy.106, bf16[8,16,128,512]{2,1,0,3:T(8,128)(2,1)} %copy.107), kind=kOutput, calls=%fused_computation.48 | convolution fusion | flops 268435456 | bytes 33555456 | tf_op jit(solution)/shard_map/xcyn,xoyn->co/dot_general | solution.py:110
  312.1 6.0 all-to-all-start.2
  318.2 8.3 %reshape.513 = bf16[12,12,8,2,16,16]{5,4,3,2,1,0:T(8,128)(2,1)} reshape(bf16[12,96,2,256]{3,2,1,0:T(2,128)(2,1)S(1)} %copy-done.7) | data formatting | bytes 2359296 | tf_op jit(solution)/shard_map/reshape | solution.py:48
  326.5 45.8 %psum.7 = f32[16,16]{1,0:T(8,128)S(1)} all-reduce(f32[16,16]{1,0:T(8,128)S(1)} %convolution_bitcast_fusion), channel_id=1, replica_groups=mesh['grp'=2,'sp'=16] {'sp'}, use_global_device_ids=true, to_apply=%region_0.1 | all-reduce | flops 256 | bytes 2048 | tf_op jit(solution)/shard_map/psum | solution.py:113
  373.0 16.5 %copy.85 = f32[16,8,12,256]{1,0,3,2:T(8,128)} copy(f32[16,8,12,256]{3,1,2,0:T(8,128)} %bitcast.20) | data formatting | bytes 3145728 | tf_op jit(solution)/shard_map/all_to_all | solution.py:88
  389.5 17.1 %reshape.512 = f32[128,12,16,2,8]{0,4,3,2,1:T(8,128)S(1)} reshape(f32[16,8,12,256]{1,0,3,2:T(8,128)} %copy.85) | data formatting | bytes 3145728 | tf_op jit(solution)/shard_map/reshape | solution.py:94
  406.6 6.6 fusion.37
  413.2 1.5 slice_bitcast_fusion.11
  415.6 9.9 %fusion.22 = f32[12,12,8,1,16]{4,3,2,1,0:T(1,128)} fusion(bf16[12,12,8,2,16,16]{5,4,3,2,1,0:T(8,128)(2,1)} %reshape.513, f32[12,12,8,16,1]{3,1,2,0,4:T(8,128)S(1)} %get-tuple-element.17), kind=kOutput, calls=%fused_computation.21 | convolution fusion | flops 3538944 | bytes 4866048 | tf_op jit(solution)/shard_map/mktco,mkto->mktc/dot_general | solution.py:55
  425.5 1.7 copy.115
  427.2 10.3 %fusion.24 = f32[12,12,8,1,16]{4,3,2,1,0:T(1,128)} fusion(bf16[12,12,8,2,16,16]{5,4,3,2,1,0:T(8,128)(2,1)} %reshape.513, f32[12,12,8,16,1]{3,1,2,0,4:T(8,128)S(1)} %get-tuple-element.18), kind=kOutput, calls=%fused_computation.23 | convolution fusion | flops 3538944 | bytes 4866048 | tf_op jit(solution)/shard_map/mktco,mkto->mktc/dot_general | solution.py:55
  437.5 1.7 copy.117
  439.2 10.1 %fusion.21 = f32[12,12,8,1,16]{4,3,2,1,0:T(1,128)} fusion(bf16[12,12,8,2,16,16]{5,4,3,2,1,0:T(8,128)(2,1)} %reshape.513, f32[12,12,8,16,1]{3,1,2,0,4:T(8,128)} %copy-done.9), kind=kOutput, calls=%fused_computation.20 | convolution fusion | flops 3538944 | bytes 5578752 | tf_op jit(solution)/shard_map/mktco,mkto->mktc/dot_general | solution.py:58
  449.3 2.4 copy.118
  451.7 10.1 %fusion.23 = f32[12,12,8,1,16]{4,3,2,1,0:T(1,128)} fusion(bf16[12,12,8,2,16,16]{5,4,3,2,1,0:T(8,128)(2,1)} %reshape.513, f32[12,12,8,16,1]{3,1,2,0,4:T(8,128)} %copy-done.8), kind=kOutput, calls=%fused_computation.22 | convolution fusion | flops 3538944 | bytes 5578752 | tf_op jit(solution)/shard_map/mktco,mkto->mktc/dot_general | solution.py:58
  461.7 2.6 copy.119
  464.3 1.7 fusion.44
  466.0 1.5 fusion.43
  468.0 2.0 copy.89
  471.1 4.8 all-to-all-start.1
  475.9 22.6 %fusion.1 = f32[8,128,512,16]{2,3,1,0:T(8,128)} fusion(bf16[8,16,128,512]{3,2,1,0:T(8,128)(2,1)} %param.9, bf16[16,16]{1,0:T(8,128)(2,1)S(1)} %copy-done), kind=kOutput, calls=%fused_computation.2 | convolution fusion | flops 268435456 | bytes 50332160 | tf_op jit(solution)/shard_map/co,xoyn->xcyn/dot_general | solution.py:106
  500.9 16.5 %copy.100 = f32[16,8,12,256]{1,0,3,2:T(8,128)} copy(f32[16,8,12,256]{3,1,2,0:T(8,128)} %bitcast.202) | data formatting | bytes 3145728 | tf_op jit(solution)/shard_map/all_to_all | solution.py:87
  517.4 18.3 %reshape.519 = f32[128,12,16,2,8]{0,4,3,2,1:T(8,128)} reshape(f32[16,8,12,256]{1,0,3,2:T(8,128)} %copy.100) | data formatting | bytes 3145728 | tf_op jit(solution)/shard_map/reshape | solution.py:91
  535.7 8.1 %fusion.40 = f32[12,12,8,2,16]{4,1,2,0,3:T(8,128)S(1)} fusion(f32[128,12,16,2,8]{0,4,3,2,1:T(8,128)} %reshape.519, f32[128,1,12,2]{0,2,1,3:T(8,128)S(1)} %get-tuple-element.23, f32[128,1,12,2]{0,2,1,3:T(8,128)S(1)} %get-tuple-element.22), kind=kOutput, calls=%fused_computation.46 | convolution fusion | flops 113252352 | bytes 1744896 | tf_op jit(solution)/shard_map/xmcpt,xpkq->mktqc/dot_general | solution.py:90
  544.4 7.0 %multiply_add_fusion = (f32[12,12,8,16,16]{4,3,2,1,0:T(8,128)}, f32[12,12,8,16,16]{4,3,2,1,0:T(8,128)}) fusion(f32[12,12,8,16]{3,2,1,0:T(8,128)S(1)} %copy-done.6, f32[12,12,8,16]{3,2,1,0:T(8,128)S(1)} %copy.104, f32[12,12,8,16]{3,2,1,0:T(8,128)S(1)} %copy.103, f32[12,12,8,16]{3,2,1,0:T(8,128)S(1)} %copy.102), kind=kLoop, calls=%fused_computation.14 | loop fusion | flops 1769472 | bytes 2654208 | tf_op jit(solution)/shard_map/add | solution.py:61
  551.4 6.9 %add.136 = f32[12,96,1,256]{3,1,0,2:T(8,128)S(1)} reshape(f32[12,12,8,16,16]{4,3,2,1,0:T(8,128)} %get-tuple-element.12) | data formatting | bytes 2359296 | tf_op jit(solution)/shard_map/add | solution.py:61
  558.2 7.8 %sub.19 = f32[12,96,1,256]{3,1,0,2:T(8,128)} reshape(f32[12,12,8,16,16]{4,3,2,1,0:T(8,128)} %get-tuple-element.13) | data formatting | bytes 2359296 | tf_op jit(solution)/shard_map/sub | solution.py:62
  566.0 1.6 pad_maximum_fusion
  567.6 3.2 copy.108
  570.9 6.9 %copy.91 = f32[8,16,12,256]{1,3,2,0:T(8,128)} copy(f32[8,16,12,256]{3,2,0,1:T(8,128)S(1)} %bitcast.201) | data formatting | bytes 3145728 | tf_op jit(solution)/shard_map/all_to_all | solution.py:100
  577.8 18.4 %fusion.15 = f32[8,16,128,2,12,8]{2,1,5,4,0,3:T(8,128)} fusion(f32[8,16,12,16,2,8]{1,5,4,3,2,0:T(8,128)} %bitcast.200, f32[128,1,16,2]{0,2,1,3:T(8,128)S(1)} %copy-done.13, f32[128,1,16,2]{0,2,1,3:T(8,128)S(1)} %copy-done.11), kind=kOutput, calls=%fused_computation.18 | convolution fusion | flops 1207967744 | bytes 14188544 | tf_op jit(solution)/shard_map/xkzcpt,yqkp->xcyqzt/dot_general | solution.py:102
  596.1 12.8 %copy.94 = f32[8,16,128,2,12,8]{2,5,4,3,1,0:T(8,128)} copy(f32[8,16,128,2,12,8]{2,1,5,4,0,3:T(8,128)} %fusion.15) | data formatting | bytes 25165824 | tf_op jit(solution)/shard_map/xkzcpt,yqkp->xcyqzt/transpose | solution.py:102
  609.0 55.3 %fusion = bf16[8,16,128,512]{3,2,1,0:T(8,128)(2,1)} fusion(f32[8,128,512,16]{2,3,1,0:T(8,128)} %fusion.1, f32[8,16,128,192]{2,3,1,0:T(8,128)} %bitcast.197, f32[512,192,1,1]{0,1,2,3:T(8,128)S(1)} %copy-done.3), kind=kOutput, calls=%fused_computation.1 | convolution fusion | flops 19344130048 | bytes 63307776 | tf_op jit(solution)/shard_map/xcym,nm->xcyn/dot_general | solution.py:105
  (51 shorter events, 9.4 us)
Async XLA Ops:
  0.6 475.3 %copy-start = (bf16[16,16]{1,0:T(8,128)(2,1)S(1)}, bf16[16,16]{1,0:T(8,128)(2,1)}, u32[]{:S(2)}) copy-start(bf16[16,16]{1,0:T(8,128)(2,1)} %param.11) | copy-start | bytes 1540
  12.6 127.1 %copy-start.2 = (f32[512,192,1,1]{0,1,2,3:T(8,128)}, f32[512,192,1,1]{0,1,2,3:T(8,128)S(1)}, u32[]{:S(2)}) copy-start(f32[512,192,1,1]{0,1,2,3:T(8,128)S(1)} %reshape.520) | copy-start | bytes 1179652
  12.6 30.0 %copy-start.14 = (f32[128,16,1]{0,1,2:T(8,128)S(1)}, f32[128,16,1]{0,1,2:T(8,128)}, u32[]{:S(2)}) copy-start(f32[128,16,1]{0,1,2:T(8,128)} %get-tuple-element.30) | copy-start | bytes 24580
  12.6 30.0 %copy-start.15 = (f32[128,16,1]{0,1,2:T(8,128)S(1)}, f32[128,16,1]{0,1,2:T(8,128)}, u32[]{:S(2)}) copy-start(f32[128,16,1]{0,1,2:T(8,128)} %get-tuple-element.31) | copy-start | bytes 24580
  42.6 164.7 %copy-start.10 = (f32[128,1,16,2]{0,2,1,3:T(8,128)}, f32[128,1,16,2]{0,2,1,3:T(8,128)S(1)}, u32[]{:S(2)}) copy-start(f32[128,1,16,2]{0,2,1,3:T(8,128)S(1)} %get-tuple-element.24) | copy-start | bytes 49156
  42.6 164.7 %copy-start.12 = (f32[128,1,16,2]{0,2,1,3:T(8,128)}, f32[128,1,16,2]{0,2,1,3:T(8,128)S(1)}, u32[]{:S(2)}) copy-start(f32[128,1,16,2]{0,2,1,3:T(8,128)S(1)} %get-tuple-element.25) | copy-start | bytes 49156
  132.3 179.7 %all-to-all-start = ((f32[8,192,256]{2,0,1:T(8,128)}), f32[8,192,256]{2,0,1:T(8,128)}, u32[]{:S(2)}, u32[]{:S(2)}) async-start(f32[8,192,256]{2,0,1:T(8,128)} %copy.84), calls=%async_computation | async-start | bytes 3145728 | tf_op jit(solution)/shard_map/all_to_all | solution.py:88
  297.9 20.1 %copy-start.16 = (s32[12]{0:T(128)S(1)}, s32[12]{0:T(128)}, u32[]{:S(2)}) copy-start(s32[12]{0:T(128)} %param.12) | copy-start | bytes 148
  297.9 20.3 %copy-start.7 = (bf16[12,96,2,256]{3,2,1,0:T(2,128)(2,1)S(1)}, bf16[12,96,2,256]{3,2,1,0:T(2,128)(2,1)}, u32[]{:S(2)}) copy-start(bf16[12,96,2,256]{3,2,1,0:T(2,128)(2,1)} %param.10) | copy-start | bytes 3538948
  312.1 157.9 %all-to-all-start.2 = ((f32[8,192,256]{2,0,1:T(8,128)}), f32[8,192,256]{2,0,1:T(8,128)S(1)}, u32[]{:S(2)}, u32[]{:S(2)}) async-start(f32[8,192,256]{2,0,1:T(8,128)} %copy.99), calls=%async_computation.2 | async-start | bytes 3145728 | tf_op jit(solution)/shard_map/all_to_all | solution.py:87
  414.7 0.9 copy-start.8
  414.7 12.5 %copy-start.9 = (f32[12,12,8,16,1]{3,1,2,0,4:T(8,128)}, f32[12,12,8,16,1]{3,1,2,0,4:T(8,128)S(1)}, u32[]{:S(2)}) copy-start(f32[12,12,8,16,1]{3,1,2,0,4:T(8,128)S(1)} %get-tuple-element.18) | copy-start | bytes 221188
  469.9 1.1 copy-start.4
  471.1 99.8 %all-to-all-start.1 = ((f32[128,12,256]{2,1,0:T(8,128)}), f32[128,12,256]{2,1,0:T(8,128)S(1)}, u32[]{:S(2)}, u32[]{:S(2)}) async-start(f32[128,12,256]{2,1,0:T(8,128)} %copy.89), calls=%async_computation.1 | async-start | bytes 4194304 | tf_op jit(solution)/shard_map/all_to_all | solution.py:100
  475.9 23.9 %copy-start.5 = (f32[12,12,8,16]{3,1,2,0:T(8,128)S(1)}, f32[12,12,8,16]{3,1,2,0:T(8,128)}, u32[]{:S(2)}) copy-start(f32[12,12,8,16]{3,1,2,0:T(8,128)} %get-tuple-element.19) | copy-start | bytes 221188
  535.7 8.7 %copy-start.6 = (f32[12,12,8,16]{3,2,1,0:T(8,128)S(1)}, f32[12,12,8,16]{3,2,1,0:T(8,128)}, u32[]{:S(2)}) copy-start(f32[12,12,8,16]{3,2,1,0:T(8,128)} %copy.105) | copy-start | bytes 221188
  567.6 10.1 %copy-start.11 = (f32[128,1,16,2]{0,2,1,3:T(8,128)S(1)}, f32[128,1,16,2]{0,2,1,3:T(8,128)}, u32[]{:S(2)}) copy-start(f32[128,1,16,2]{0,2,1,3:T(8,128)} %copy-done.10) | copy-start | bytes 49156
  567.6 10.1 %copy-start.13 = (f32[128,1,16,2]{0,2,1,3:T(8,128)S(1)}, f32[128,1,16,2]{0,2,1,3:T(8,128)}, u32[]{:S(2)}) copy-start(f32[128,1,16,2]{0,2,1,3:T(8,128)} %copy-done.12) | copy-start | bytes 49156
  596.1 12.8 %copy-start.3 = (f32[512,192,1,1]{0,1,2,3:T(8,128)S(1)}, f32[512,192,1,1]{0,1,2,3:T(8,128)}, u32[]{:S(2)}) copy-start(f32[512,192,1,1]{0,1,2,3:T(8,128)} %copy-done.2) | copy-start | bytes 1179652
  609.0 55.3 %copy-start.1 = (bf16[16,16]{1,0:T(8,128)(2,1)S(1)}, bf16[16,16]{1,0:T(8,128)(2,1)}, u32[]{:S(2)}) copy-start(bf16[16,16]{1,0:T(8,128)(2,1)} %param.11) | copy-start | bytes 1540
where the time goes:
time: 675 us; the launch traced here: 664 us
  matrix products  327 us (48%)
  local copies, waits for them, and re-layouts  252 us (37%)
  blocking collectives  45.8 us (7%)
  other arithmetic  20.5 us (3%)
  starting transfers between devices  18.3 us (3%)
    dot_general x2, matrix products, local_spectra(): spectra = jnp.einsum('xcypzt,ypkq->xkzcqt', planes_zt, ytab, precision=HIGH)  109 us
    dot_general x1, matrix products, shards(): spectral = jnp.einsum('xcym,nm->xcyn', planes_zt, plane, precision=HIGH)  55.3 us
    unnamed x37, local copies, waits for them, and re-layouts  52.1 us
    dot_general x2, matrix products, local_spectra(): jnp.einsum('xcyn,nm->xcym', field, plane, precision=HIGH, preferred_eleme...  50.8 us
    psum x1, blocking collectives, shards(): total = lax.psum(partial_total, 'sp')  45.8 us
    transpose x2, local copies, waits for them, and re-layouts, local_spectra(): spectra = jnp.einsum('xcypzt,ypkq->xkzcqt', planes_zt, ytab, precision=HIGH)  43.4 us
    reshape x4, local copies, waits for them, and re-layouts, local_spectra(): return spectra.reshape(slab_rows, KY * KZ, C * 2 * KT)  27.8 us
    dot_general x1, matrix products, shards(): jnp.einsum('co,xoyn->xcyn', bypass_weight, out_grad, preferred_element_ty...  22.6 us
  transfers between devices with their start and end apart: 3, of which 0 were waited for; matrix products, arithmetic and copies ran while one was open for 56% of the time, Pallas kernels for 0%

commit v1 on v0

v1 whole, which is shorter than its diff:
```python
import functools
import math

import jax
import jax.numpy as jnp
from jax import lax
from jax.experimental import pallas as pl
from jax.experimental.pallas import tpu as pltpu
from jax.sharding import PartitionSpec as P

F32 = jnp.float32
BF16 = jnp.bfloat16
LANES = 128
NT = (((1,), (1,)), ((), ()))
NN = (((1,), (0,)), ((), ()))


def mm(a, b, dims=NN):
    return lax.dot_general(a, b, dims, preferred_element_type=F32)


def split(a):
    hi = a.astype(BF16)
    return hi, (a - hi.astype(F32)).astype(BF16)


def mm3(a_hi, a_lo, b_hi, b_lo, dims=NN):
    return mm(a_hi, b_hi, dims) + (mm(a_hi, b_lo, dims) + mm(a_lo, b_hi, dims))


def split_table(table):
    hi = lax.reduce_precision(table, 8, 7)
    return hi.astype(BF16), (table - hi).astype(BF16)


def params(**kw):
    return pltpu.CompilerParams(vmem_limit_bytes=48 * 1024 * 1024, **kw)


def spectra_step(field, ty, p_hi, p_lo, a_hi, a_lo, s_all, step):
    chans = field.shape[1]
    ky = ty.shape[0] // 4
    width = field.shape[3]
    for c in range(chans):
        both = mm(ty[...], field[0, c])
        part = both[: 2 * ky] + both[2 * ky :]
        hi, lo = split(part)
        rows = slice(c * ky, (c + 1) * ky)
        a_hi[rows, :width] = hi[:ky]
        a_hi[rows, width:] = hi[ky:]
        a_lo[rows, :width] = lo[:ky]
        a_lo[rows, width:] = lo[ky:]
    res = mm3(a_hi[...], a_lo[...], p_hi[...], p_lo[...])
    for p in range(2):
        s_all[step, p] = res[:, p * LANES : (p + 1) * LANES]


def spectra_end(m_hi, m_lo, out, s_all, ky, used):
    slabs, _, rows, _ = s_all.shape
    chans = rows // ky

    def one(j, carry):
        pieces = [
            s_all[x, p, pl.ds(j, chans, stride=ky), :]
            for p in range(2)
            for x in range(slabs)
        ]
        s_t = jnp.concatenate(pieces, axis=0).T
        hi, lo = split(s_t)
        res = mm3(hi, lo, m_hi[...], m_lo[...])
        out[pl.ds(pl.multiple_of(j * used, 8), used), :] = res[:used]
        return carry

    lax.fori_loop(0, ky, one, 0, unroll=2)


def forward_kernel(field, ty, p_hi, p_lo, m_hi, m_lo, out, a_hi, a_lo, s_all, *, used):
    step = pl.program_id(0)
    spectra_step(field, ty, p_hi, p_lo, a_hi, a_lo, s_all, step)

    @pl.when(step == pl.num_programs(0) - 1)
    def _():
        spectra_end(m_hi, m_lo, out, s_all, ty.shape[0] // 4, used)


def forward_both_kernel(
    field, grad, ty, p_hi, p_lo, m_hi, m_lo, out, gram_out, a_hi, a_lo, s_all, gram, *, used
):
    step = pl.program_id(0)
    chans, height, width = field.shape[1:]
    blk = 16

    @pl.when(step == 0)
    def _():
        gram[...] = jnp.zeros_like(gram)

    spectra_step(field, ty, p_hi, p_lo, a_hi, a_lo, s_all, step)
    total = gram[...]
    for b in range(height // blk):
        rows = slice(b * blk, (b + 1) * blk)
        left = field[0, :, rows, :].reshape(chans * blk, width)
        right = grad[0, :, rows, :].reshape(chans * blk, width)
        total = total + mm(left, right, NT)
    gram[...] = total

    @pl.when(step == pl.num_programs(0) - 1)
    def _():
        spectra_end(m_hi, m_lo, out, s_all, ty.shape[0] // 4, used)
        gram_out[...] = gram[...]


def whole(shape):
    return pl.BlockSpec(shape, lambda *_: (0,) * len(shape), pipeline_mode=pl.Buffered(1))


def forward(fields, tabs, used):
    slabs, chans, height, width = fields[0].shape
    ty, p_hi, p_lo, m_hi, m_lo = tabs
    ky = ty.shape[0] // 4
    with_gram = len(fields) == 2
    block = pl.BlockSpec((1, chans, height, width), lambda i: (i, 0, 0, 0))
    outs = [jax.ShapeDtypeStruct((ky * used, m_hi.shape[1]), F32)]
    scratch = [
        pltpu.VMEM((chans * ky, 2 * width), BF16),
        pltpu.VMEM((chans * ky, 2 * width), BF16),
        pltpu.VMEM((slabs, 2, chans * ky, LANES), F32),
    ]
    if with_gram:
        outs.append(jax.ShapeDtypeStruct((chans * 16, chans * 16), F32))
        scratch.append(pltpu.VMEM((chans * 16, chans * 16), F32))
    kernel = forward_both_kernel if with_gram else forward_kernel
    res = pl.pallas_call(
        functools.partial(kernel, used=used),
        grid=(slabs,),
        in_specs=[block] * len(fields) + [whole(t.shape) for t in tabs],
        out_specs=[whole(o.shape) for o in outs],
        out_shape=outs,
        scratch_shapes=scratch,
        compiler_params=params(),
        name="forward_both" if with_gram else "forward_one",
        cost_estimate=pl.CostEstimate(
            flops=int(2e10), bytes_accessed=2 * sum(f.size for f in fields), transcendentals=0
        ),
    )(*fields, *tabs)
    return res if with_gram else res[0]


def mix_kernel(g, w_re, w_im, spread, gather, out):
    kx, kt = w_re.shape[1], w_re.shape[2]
    modes, chans2 = w_re.shape[0], w_re.shape[3]
    rows = modes * kt
    per = LANES // 16
    nblk = g.shape[1] // LANES
    acc = [jnp.zeros((rows, LANES), F32) for _ in range(nblk)]
    halves = []
    for b in range(nblk):
        hi, lo = split(g[:, b * LANES : (b + 1) * LANES])
        halves.append(jnp.concatenate([hi, lo], axis=1))
    for k in range(kx):
        i_re, i_im = k, kx + k
        e_re = mm(halves[i_re // per], spread[i_re % per])
        e_im = mm(halves[i_im // per], spread[i_im % per])
        wr = w_re[:, k].reshape(rows, chans2).astype(F32)
        wi = w_im[:, k].reshape(rows, chans2).astype(F32)
        for q, prod in ((i_re, wr * e_re + wi * e_im), (i_im, wr * e_im - wi * e_re)):
            hi, lo = split(prod)
            mat = gather[q % per]
            acc[q // per] = acc[q // per] + (mm(hi, mat) + mm(lo, mat))
    for b in range(nblk):
        out[:, b * LANES : (b + 1) * LANES] = acc[b]


def mix(g, w_re, w_im, spread, gather):
    return pl.pallas_call(
        mix_kernel,
        out_shape=jax.ShapeDtypeStruct(g.shape, F32),
        compiler_params=params(),
        name="mix",
        cost_estimate=pl.CostEstimate(flops=int(1e9), bytes_accessed=4 * 10**6, transcendentals=0),
    )(g, w_re, w_im, spread, gather)


def wgrad_kernel(u, g, spread_c, spread_o, out_re, out_im):
    modes, kx, kt, _ = out_re.shape
    per = LANES // 16
    nblk = g.shape[1] // LANES
    halves = []
    for ref in (u, g):
        parts = []
        for b in range(nblk):
            hi, lo = split(ref[:, b * LANES : (b + 1) * LANES])
            parts.append(jnp.concatenate([hi, lo], axis=1))
        halves.append(parts)
    for k in range(kx):
        i_re, i_im = k, kx + k
        u_re = mm(halves[0][i_re // per], spread_c[i_re % per])
        u_im = mm(halves[0][i_im // per], spread_c[i_im % per])
        g_re = mm(halves[1][i_re // per], spread_o[i_re % per])
        g_im = mm(halves[1][i_im // per], spread_o[i_im % per])
        out_re[:, k] = (u_re * g_re + u_im * g_im).reshape(modes, kt, -1)
        out_im[:, k] = (u_re * g_im - u_im * g_re).reshape(modes, kt, -1)


def wgrad(u, g, spread_c, spread_o, shape):
    return pl.pallas_call(
        wgrad_kernel,
        out_shape=[jax.ShapeDtypeStruct(shape, F32)] * 2,
        compiler_params=params(),
        name="wgrad",
        cost_estimate=pl.CostEstimate(flops=int(1e9), bytes_accessed=4 * 10**6, transcendentals=0),
    )(u, g, spread_c, spread_o)


def inverse_kernel(
    grad, adj, m_hi, m_lo, pi_hi, pi_lo, tyi, bmat, out, l_all, acc, *, used, slabs
):
    step = pl.program_id(0)
    chans, height, width = grad.shape[1:]
    ky = adj.shape[0] // used
    blk = 16

    @pl.when(step == 0)
    def _():
        def one(jj, carry):
            rows = []
            for i in range(2):
                start = pl.multiple_of((2 * jj + i) * used, 8)
                rows.append(adj[pl.ds(start, used), :])
                if used < LANES:
                    rows.append(jnp.zeros((LANES - used, adj.shape[1]), F32))
            hi, lo = split(jnp.concatenate(rows, axis=0))
            h = mm3(m_hi[...], m_lo[...], hi, lo, NT)
            for i in range(2):
                for p in range(2):
                    for x in range(slabs):
                        r = (p * slabs + x) * chans
                        l_all[x, p, pl.ds(2 * jj + i, chans, stride=ky), :] = h[
                            r : r + chans, i * LANES : (i + 1) * LANES
                        ]
            return carry

        lax.fori_loop(0, ky // 2, one, 0)

    for b in range(height // blk):
        rows = slice(b * blk, (b + 1) * blk)
        right = grad[0, :, rows, :].reshape(chans * blk, width)
        acc[:, rows, :] = mm(bmat[...], right).reshape(chans, blk, width)
    l_hi, l_lo = split(jnp.concatenate([l_all[step, 0], l_all[step, 1]], axis=1))
    h2 = mm3(l_hi, l_lo, pi_hi[...], pi_lo[...])
    for c in range(chans):
        rows = slice(c * ky, (c + 1) * ky)
        re_hi, re_lo = split(h2[rows, :width])
        im_hi, im_lo = split(h2[rows, width:])
        rhs = jnp.concatenate([re_hi, im_hi, re_lo, im_lo, re_hi, im_hi], axis=0)
        out[0, c] = (acc[c] + mm(tyi[...], rhs)).astype(out.dtype)


def inverse(grad, adj, m_hi, m_lo, pi_hi, pi_lo, tyi, bmat, used):
    slabs, chans, height, width = grad.shape
    ky = adj.shape[0] // used
    block = pl.BlockSpec((1, chans, height, width), lambda i: (i, 0, 0, 0))
    rest = (adj, m_hi, m_lo, pi_hi, pi_lo, tyi, bmat)
    return pl.pallas_call(
        functools.partial(inverse_kernel, used=used, slabs=slabs),
        grid=(slabs,),
        in_specs=[block] + [whole(t.shape) for t in rest],
        out_specs=block,
        out_shape=jax.ShapeDtypeStruct(grad.shape, grad.dtype),
        scratch_shapes=[
            pltpu.VMEM((slabs, 2, chans * ky, LANES), F32),
            pltpu.VMEM((chans, height, width), F32),
        ],
        compiler_params=params(),
        name="inverse",
        cost_estimate=pl.CostEstimate(
            flops=int(3e10), bytes_accessed=4 * grad.size, transcendentals=0
        ),
    )(grad, *rest)


def bits_of(pos, order):
    k = len(order)
    return sum(((pos >> (k - 1 - s)) & 1) << bit for s, bit in enumerate(order))


def relabel(modes, own, order):
    n = 1 << len(order)
    if n == 1:
        return modes
    per = modes.shape[0] // n
    offs = jnp.array([bits_of(p, order) for p in range(n)], jnp.int32)
    blocks = own ^ offs
    idx = (blocks[:, None] * per + jnp.arange(per, dtype=jnp.int32)[None, :]).reshape(-1)
    hit = idx[:, None] == jnp.arange(modes.shape[0], dtype=jnp.int32)[None, :]
    return jnp.sum(jnp.where(hit, modes[None, :], 0), axis=1)


def trig(phase, length):
    angles = 2.0 * math.pi / length * phase.astype(F32)
    return jnp.cos(angles), jnp.sin(angles)


def y_table(modes, length):
    pos = jnp.arange(length, dtype=jnp.int32)
    c, s = trig(modes[:, None] * pos[None, :] % length, length)
    f = 1.0 / math.sqrt(length)
    return jnp.concatenate([c, -s], axis=0) * f


def plane_tables(modes_z, modes_t, nz, nt):
    used = modes_z.shape[0] * modes_t.shape[0]
    mz = jnp.repeat(modes_z, modes_t.shape[0])
    mt = jnp.tile(modes_t, modes_z.shape[0])
    pos = jnp.arange(nz * nt, dtype=jnp.int32)
    z, t = pos // nt, pos % nt
    f = 1.0 / math.sqrt(nz * nt)
    tabs = []
    for flip in (False, True):
        if flip:
            ph = (mz[:, None] * z[None, :] % nz) * nt + (mt[:, None] * t[None, :] % nt) * nz
        else:
            ph = (z[:, None] * mz[None, :] % nz) * nt + (t[:, None] * mt[None, :] % nt) * nz
        c, s = trig(ph % (nz * nt), nz * nt)
        pad = [(0, LANES - used), (0, 0)] if flip else [(0, 0), (0, LANES - used)]
        c, s = lax.optimization_barrier((jnp.pad(c * f, pad), jnp.pad(s * f, pad)))
        if flip:
            full = jnp.concatenate(
                [jnp.concatenate([c, s], axis=1), jnp.concatenate([-s, c], axis=1)], axis=0
            )
        else:
            full = jnp.concatenate(
                [jnp.concatenate([c, -s], axis=1), jnp.concatenate([s, c], axis=1)], axis=0
            )
        tabs.append(split_table(full))
    return tabs


def x_table(modes, first, slabs, length, chans):
    pos = first + jnp.arange(slabs, dtype=jnp.int32)
    c, s = trig(pos[:, None] * modes[None, :] % length, length)
    f = 1.0 / math.sqrt(length)
    c, s = lax.optimization_barrier((c * f, s * f))
    core = jnp.stack([jnp.stack([c, -s], axis=1), jnp.stack([s, c], axis=1)], axis=0)
    eye = jnp.eye(chans, dtype=F32)
    full = core[:, :, None, :, :, None] * eye[None, None, :, None, None, :]
    kx = modes.shape[0]
    return split_table(full.reshape(2 * slabs * chans, 2 * kx * chans))


def spread_tables(chans):
    per = LANES // chans
    src = jnp.arange(LANES)
    dst = jnp.arange(chans * chans)
    grp = jnp.arange(per)
    inside = (src[None, :, None] // chans) == grp[:, None, None]
    by_c = inside & (src[None, :, None] % chans == dst[None, None, :] // chans)
    by_o = inside & (src[None, :, None] % chans == dst[None, None, :] % chans)
    twice = lambda a: jnp.concatenate([a, a], axis=1).astype(BF16)
    gather = jnp.swapaxes(by_c, 1, 2).astype(BF16)
    return twice(by_c), twice(by_o), gather


def flips(n, bit):
    return [(i, i ^ (1 << bit)) for i in range(n)]


def reduce_blocks(parts, order, n):
    data, *small = parts
    for bit in order:
        half = data.shape[0] // 2
        got = lax.ppermute(data[half:], "sp", flips(n, bit))
        data = data[:half] + got
        small = [s + lax.ppermute(s, "sp", flips(n, bit)) for s in small]
    return [data, *small]


def gather_blocks(data, order, n):
    for bit in reversed(order):
        data = jnp.concatenate([data, lax.ppermute(data, "sp", flips(n, bit))], axis=0)
    return data


def shards(
    n, field_in, out_grad, spectral_weight, bypass_weight, mode_x, mode_y, mode_z, mode_t
):
    slabs, chans, height, width = field_in.shape
    kx, ky, kz, kt = (m.shape[0] for m in (mode_x, mode_y, mode_z, mode_t))
    modes_dev = spectral_weight.shape[0]
    length = slabs * n
    own = lax.axis_index("sp").astype(jnp.int32)
    nbits = n.bit_length() - 1
    low = max(0, nbits - (ky.bit_length() - 1))
    order_y = list(range(nbits - low))
    order_z = list(range(low))
    order = [b + low for b in order_y] + order_z
    my = relabel(mode_y, own >> low, order_y)
    mz = relabel(mode_z, own & ((1 << low) - 1), order_z)
    used = kz * kt
    nt = 16
    nz = width // nt

    ty = y_table(my, height)
    ty_hi, ty_lo = split_table(ty)
    tyf = jnp.concatenate([ty_hi, ty_lo], axis=0)
    tyi = jnp.concatenate([ty_hi.T, ty_hi.T, ty_lo.T], axis=1)
    (p_hi, p_lo), (pi_hi, pi_lo) = plane_tables(mz, mode_t, nz, nt)
    m_hi, m_lo = x_table(mode_x, own * slabs, slabs, length, chans)
    by_c, by_o, summed = spread_tables(chans)
    bmat = (
        bypass_weight[:, None, :, None] * jnp.eye(16, dtype=BF16)[None, :, None, :]
    ).reshape(chans * 16, chans * 16)
    tabs = (tyf, p_hi, p_lo, m_hi, m_lo)

    part_g = forward((out_grad,), tabs, used)
    (spec_g,) = reduce_blocks([part_g], order, n)
    part_u, gram = forward((field_in, out_grad), tabs, used)
    diag = jnp.trace(gram.reshape(chans, 16, chans, 16), axis1=1, axis2=3)

    wm = spectral_weight.reshape(modes_dev, kx, kt, 2, chans * chans)
    w_re, w_im = wm[:, :, :, 0], wm[:, :, :, 1]
    adj = mix(spec_g, w_re, w_im, by_o, summed)
    spec_u, total = reduce_blocks([part_u, diag], order, n)
    adj_all = gather_blocks(adj, order, n)
    in_grad = inverse(out_grad, adj_all, m_hi, m_lo, pi_hi, pi_lo, tyi, bmat, used)
    g_re, g_im = wgrad(spec_u, spec_g, by_c, by_o, (modes_dev, kx, kt, chans * chans))
    weight_grad = jnp.stack([g_re, g_im], axis=3).reshape(modes_dev, kx * kt, 2, chans * chans)
    bypass_grad = total / math.sqrt(length * height * width)
    return (in_grad, weight_grad, bypass_grad)


def solution(mesh):
    rows = P(("grp", "sp"), None, None, None)
    return jax.shard_map(
        functools.partial(shards, mesh.shape["sp"]),
        mesh=mesh,
        in_specs=(rows, rows, P("sp", None, None, None), P(), P(), P(), P(), P()),
        out_specs=(rows, rows, P("grp", None)),
        check_vma=False,
    )
```

time: 675 us -> 177 us (0.26); the launches traced: 664 us -> 177 us
  matrix products: 327 us -> 0 us
  local copies, waits for them, and re-layouts: 252 us -> 21 us
  Pallas kernels: 0 us -> 62.3 us
  waiting for transfers between devices: 0.01 us -> 50.2 us
  blocking collectives: 45.8 us -> 0 us
    dot_general x15 -> x0, matrix products: 327 us -> none  [the longest x2 109 us: local_spectra(): spectra = jnp.einsum('xcypzt,ypkq->xkzcqt', planes_zt, ytab, precision=HIGH)]
    reshape x8 -> x1, local copies, waits for them, and re-layouts: 73.5 us -> 1.98 us  [shards(): diag = jnp.trace(gram.reshape(chans, 16, chans, 16), axis1=1, axis2=3)]
    pallas_call x0 -> x5, Pallas kernels: none -> 62.3 us  [the longest x2 36 us: forward(): pl.pallas_call(functools.partial(kernel, used=used), grid=(slabs,), in_sp...]
    transpose x4 -> x0, local copies, waits for them, and re-layouts: 56.7 us -> none  [the longest x2 43.4 us: local_spectra(): spectra = jnp.einsum('xcypzt,ypkq->xkzcqt', planes_zt, ytab, precision=HIGH)]
    ppermute x0 -> x16, waiting for transfers between devices: none -> 50.2 us  [the longest x8 25.9 us: reduce_blocks(): got = lax.ppermute(data[half:], 'sp', flips(n, bit))]
    unnamed x37 -> x39, local copies, waits for them, and re-layouts: 52.1 us -> 3.65 us
    psum x1 -> x0, blocking collectives: 45.8 us -> none  [shards(): total = lax.psum(partial_total, 'sp')]
    all_to_all x3 -> x0, local copies, waits for them, and re-layouts: 39.9 us -> none  [the longest x1 16.5 us: shards(): lax.all_to_all(local_u, 'sp', split_axis=1, concat_axis=0, tiled=True)]
  transfers between devices with their start and end apart: 3 -> 16, of which waited for: 0 -> 8; matrix products, arithmetic and copies ran while one was open for 56% -> 18% of each run, Pallas kernels for 0% -> 14%
where the time goes in v1:
time: 177 us
  Pallas kernels  62.3 us (35%)
  waiting for transfers between devices  50.2 us (28%)
  other arithmetic  24.3 us (14%)
  local copies, waits for them, and re-layouts  21 us (12%)
  starting transfers between devices  17.5 us (10%)
    pallas_call x2, Pallas kernels, forward(): pl.pallas_call(functools.partial(kernel, used=used), grid=(slabs,), in_sp...  36 us
    ppermute x8, waiting for transfers between devices, reduce_blocks(): got = lax.ppermute(data[half:], 'sp', flips(n, bit))  25.9 us
    pallas_call x1, Pallas kernels, inverse(): pl.pallas_call(functools.partial(inverse_kernel, used=used, slabs=slabs),...  22.5 us
    ppermute x4, waiting for transfers between devices, gather_blocks(): lax.ppermute(data, 'sp', flips(n, bit))  13.9 us
    ppermute x8, starting transfers between devices, reduce_blocks(): got = lax.ppermute(data[half:], 'sp', flips(n, bit))  12.6 us
    ppermute x4, waiting for transfers between devices, reduce_blocks(): small = [s + lax.ppermute(s, 'sp', flips(n, bit)) for s in small]  10.3 us
    add x8, other arithmetic, reduce_blocks(): data = data[:half] + got  5.02 us
    slice x8, local copies, waits for them, and re-layouts, reduce_blocks(): got = lax.ppermute(data[half:], 'sp', flips(n, bit))  3.96 us
  transfers between devices with their start and end apart: 16, of which 8 were waited for; matrix products, arithmetic and copies ran while one was open for 18% of the time, Pallas kernels for 14%

profile of v1, /device:TPU:0, one launch (start us, length us, event | category | flops | bytes accessed | tf_op | source)
XLA Modules:
  0.0 176.6 jit_solution(6562713790546534045)
XLA Ops:
  3.8 0.8 select_reduce_fusion.1
  4.8 1.4 sine_multiply_fusion
  7.9 2.1 %mul.220 = f32[256,384]{0,1:T(8,128)} reshape(f32[2,8,16,2,12,16]{2,1,0,5,4,3:T(8,128)S(1)} %broadcast_multiply_fusion) | data formatting | bytes 786432 | tf_op jit(solution)/shard_map/mul | solution.py:345
  10.0 1.2 copy.27
  11.2 1.4 fusion
  12.6 15.4 %forward_one.1 = f32[1536,384]{1,0:T(8,128)S(1)} custom-call(bf16[8,16,128,512]{3,2,1,0:T(8,128)(2,1)} %grad.3, bf16[64,128]{1,0:T(8,128)(2,1)S(1)} %pad_maximum_fusion.5.ty, bf16[1024,256]{1,0:T(8,128)(2,1)S(1)} %get-tuple-element.28.p_hi, bf16[1024,256]{1,0:T(8,128)(2,1)S(1)} %get-tuple-element.27.p_lo, bf16[256,384]{1,0:T(8,128)(2,1)S(1)} %get-tuple-element.30.m_hi, ...), custom_call_target="tpu_custom_call" | custom-call | flops 20000000000 | bytes 16777216 | tf_op jit(solution)/shard_map/forward_one/pallas_call | solution.py:132
  28.1 1.2 slice.73
  29.7 20.6 %forward_both.1 = (f32[1536,384]{1,0:T(8,128)S(1)}, f32[256,256]{1,0:T(8,128)S(1)}) custom-call(bf16[8,16,128,512]{3,2,1,0:T(8,128)(2,1)} %field.3, bf16[8,16,128,512]{3,2,1,0:T(8,128)(2,1)} %grad.3, bf16[64,128]{1,0:T(8,128)(2,1)S(1)} %pad_maximum_fusion.5.ty, bf16[1024,256]{1,0:T(8,128)(2,1)S(1)} %get-tuple-element.28.p_hi, ...), custom_call_target="tpu_custom_call" | custom-call | flops 20000000000 | bytes 33554432 | tf_op jit(solution)/shard_map/forward_both/pallas_call | solution.py:132
  50.4 1.1 slice.65
  51.6 2.0 %reshape.290 = f32[16,16,16,16]{3,2,1,0:T(8,128)} reshape(f32[256,256]{1,0:T(8,128)S(1)} %get-tuple-element.22) | data formatting | bytes 524288 | tf_op jit(solution)/shard_map/reshape | solution.py:417
  53.6 2.0 %select_reduce_fusion = f32[16,16]{1,0:T(8,128)S(1)} fusion(f32[16,16,16,16]{3,2,1,0:T(8,128)} %reshape.290, pred[16,16]{1,0:T(8,128)(4,1)S(1)} %copy.34), kind=kLoop, calls=%fused_computation.1 | loop fusion | flops 130816 | bytes 263424 | tf_op jit(solution)/shard_map/jit(trace)/reduce_sum | solution.py:417
  56.3 1.0 broadcast_and_fusion
  57.3 1.4 slice_add_fusion
  58.7 2.6 %collective-permute-start.1 = (f32[384,384]{1,0:T(8,128)S(1)}, f32[384,384]{1,0:T(8,128)S(1)}, u32[]{:S(2)}, u32[]{:S(2)}) collective-permute-start(f32[384,384]{1,0:T(8,128)S(1)} %slice.75), channel_id=1, source_target_pairs={{0,2},{1,3},{2,0},{3,1},{4,6},{5,7},{6,4},{7,5},{8,10},{9,11},{10,... | collective-permute-start | bytes 1769480 | tf_op jit(solution)/shard_map/ppermute | solution.py:371
  61.6 0.9 and_convert_fusion.gather
  62.5 12.8 %collective-permute-done.1 = f32[384,384]{1,0:T(8,128)S(1)} collective-permute-done((f32[384,384]{1,0:T(8,128)S(1)}, f32[384,384]{1,0:T(8,128)S(1)}, u32[]{:S(2)}, u32[]{:S(2)}) %collective-permute-start.1) | collective-permute-done | bytes 589856 | tf_op jit(solution)/shard_map/ppermute | solution.py:371
  75.4 0.8 copy-done.13
  77.0 1.8 %collective-permute-start.2 = (f32[192,384]{1,0:T(8,128)}, f32[192,384]{1,0:T(8,128)}, u32[]{:S(2)}, u32[]{:S(2)}) collective-permute-start(f32[192,384]{1,0:T(8,128)} %slice.77), channel_id=1, source_target_pairs={{0,4},{1,5},{2,6},{3,7},{4,0},{5,1},{6,2},{7,3},{8,12},{9,13},{10,... | collective-permute-start | bytes 884744 | tf_op jit(solution)/shard_map/ppermute | solution.py:371
  78.8 1.5 copy.36
  80.5 5.6 %collective-permute-done.2 = f32[192,384]{1,0:T(8,128)} collective-permute-done((f32[192,384]{1,0:T(8,128)}, f32[192,384]{1,0:T(8,128)}, u32[]{:S(2)}, u32[]{:S(2)}) %collective-permute-start.2) | collective-permute-done | bytes 294944 | tf_op jit(solution)/shard_map/ppermute | solution.py:371
  86.1 1.0 slice_add_fusion.5
  87.1 2.6 %collective-permute-start.3 = (f32[96,384]{1,0:T(8,128)S(1)}, f32[96,384]{1,0:T(8,128)S(1)}, u32[]{:S(2)}, u32[]{:S(2)}) collective-permute-start(f32[96,384]{1,0:T(8,128)S(1)} %slice.79), channel_id=1, source_target_pairs={{0,8},{1,9},{2,10},{3,11},{4,12},{5,13},{6,14},{7,15},{8,0},{9,1},... | collective-permute-start | bytes 442376 | tf_op jit(solution)/shard_map/ppermute | solution.py:371
  89.7 1.4 slice_add_fusion.1
  91.2 1.6 collective-permute-start.9
  92.7 3.3 %collective-permute-done.3 = f32[96,384]{1,0:T(8,128)S(1)} collective-permute-done((f32[96,384]{1,0:T(8,128)S(1)}, f32[96,384]{1,0:T(8,128)S(1)}, u32[]{:S(2)}, u32[]{:S(2)}) %collective-permute-start.3) | collective-permute-done | bytes 147488 | tf_op jit(solution)/shard_map/ppermute | solution.py:371
  96.0 2.6 %mix.1 = f32[96,384]{1,0:T(8,128)S(1)} custom-call(f32[96,384]{1,0:T(8,128)S(1)} %slice_add_fusion.7.g, bf16[12,12,8,256]{3,2,1,0:T(8,128)(2,1)S(1)} %get-tuple-element.24.w_re, bf16[12,12,8,256]{3,2,1,0:T(8,128)(2,1)S(1)} %get-tuple-element.23.w_im, bf16[8,256,256]{2,1,0:T(8,128)(2,1)S(1)} %add_convert_fusion.spread.spread_o, bf16[8,256,128]{2,1,0:T(8,128)(2,1)S(1)} %copy-done.2), custom_call_target="tpu_custom_call" | custom-call | flops 1000000000 | bytes 4000000 | tf_op jit(solution)/shard_map/mix/pallas_call | solution.py:174
  98.7 1.1 broadcast_multiply_fusion.1
  99.9 8.0 %collective-permute-done.4 = f32[96,384]{1,0:T(8,128)S(1)} collective-permute-done((f32[96,384]{1,0:T(8,128)S(1)}, f32[96,384]{1,0:T(8,128)S(1)}, u32[]{:S(2)}, u32[]{:S(2)}) %collective-permute-start.4) | collective-permute-done | bytes 147488 | tf_op jit(solution)/shard_map/ppermute | solution.py:379
  108.0 1.0 sine_multiply_fusion.1
  109.1 0.8 slice.85
  109.9 2.0 %collective-permute-start.10 = (f32[192,384]{1,0:T(8,128)}, f32[192,384]{1,0:T(8,128)}, u32[]{:S(2)}, u32[]{:S(2)}) collective-permute-start(f32[192,384]{1,0:T(8,128)} %slice.85), channel_id=1, source_target_pairs={{0,4},{1,5},{2,6},{3,7},{4,0},{5,1},{6,2},{7,3},{8,12},{9,13},{10,... | collective-permute-start | bytes 884744 | tf_op jit(solution)/shard_map/ppermute | solution.py:371
  111.9 5.9 %collective-permute-done.5 = f32[192,384]{1,0:T(8,128)S(1)} collective-permute-done((f32[192,384]{1,0:T(8,128)S(1)}, f32[192,384]{1,0:T(8,128)S(1)}, u32[]{:S(2)}, u32[]{:S(2)}) %collective-permute-start.5) | collective-permute-done | bytes 294944 | tf_op jit(solution)/shard_map/ppermute | solution.py:379
  117.9 0.9 pad_maximum_fusion.2
  118.8 0.8 collective-permute-start.6
  119.9 1.3 collective-permute-start.13
  121.3 10.2 %collective-permute-done.13 = f32[16,16]{1,0:T(8,128)S(1)} collective-permute-done((f32[16,16]{1,0:T(8,128)S(1)}, f32[16,16]{1,0:T(8,128)S(1)}, u32[]{:S(2)}, u32[]{:S(2)}) %collective-permute-start.13) | collective-permute-done | bytes 1056 | tf_op jit(solution)/shard_map/ppermute | solution.py:373
  132.2 2.8 %mul.237.bmat = bf16[256,256]{1,0:T(8,128)(2,1)} reshape(bf16[16,16,16,16]{3,2,1,0:T(8,128)(2,1)} %broadcast_multiply_fusion.1) | data formatting | bytes 262144 | tf_op jit(solution)/shard_map/mul | solution.py:410
  135.2 1.6 collective-permute-start.15
  136.7 1.1 slice_add_fusion.4
  137.8 1.4 collective-permute-start.11
  139.3 1.3 pad_maximum_fusion.1
  141.2 4.3 %collective-permute-done.11 = f32[96,384]{1,0:T(8,128)S(1)} collective-permute-done((f32[96,384]{1,0:T(8,128)S(1)}, f32[96,384]{1,0:T(8,128)S(1)}, u32[]{:S(2)}, u32[]{:S(2)}) %collective-permute-start.11) | collective-permute-done | bytes 147488 | tf_op jit(solution)/shard_map/ppermute | solution.py:371
  145.5 1.1 wgrad.1
  146.7 1.2 copy.32
  147.9 1.2 copy.33
  149.2 3.5 %pad_maximum_fusion = f32[12,96,2,256]{3,2,1,0:T(2,128)} fusion(f32[12,96,1,256]{3,2,1,0:T(1,128)S(1)} %copy.33, f32[12,96,1,256]{3,2,1,0:T(1,128)S(1)} %copy.32), kind=kLoop, calls=%fused_computation | loop fusion | flops 589824 | bytes 4718592 | tf_op jit(solution)/shard_map/stack | solution.py:426
  152.7 1.2 constant_dynamic-update-slice_fusion.1
  154.1 22.5 %inverse.1 = bf16[8,16,128,512]{3,2,1,0:T(8,128)(2,1)} custom-call(bf16[8,16,128,512]{3,2,1,0:T(8,128)(2,1)} %grad.3, f32[1536,384]{1,0:T(8,128)S(1)} %constant_dynamic-update-slice_fusion.adj, bf16[256,384]{1,0:T(8,128)(2,1)S(1)} %copy-done.6, bf16[256,384]{1,0:T(8,128)(2,1)S(1)} %copy-done.4, bf16[256,1024]{1,0:T(8,128)(2,1)S(1)} %get-tuple-element.26.pi_hi, ...), custom_call_target="tpu_custom_call" | custom-call | flops 30000001024 | bytes 33554432 | tf_op jit(solution)/shard_map/inverse/pallas_call | solution.py:263
  (107 shorter events, 10.0 us)
Async XLA Ops:
  11.2 18.5 %copy-start.3 = (bf16[256,384]{1,0:T(8,128)(2,1)}, bf16[256,384]{1,0:T(8,128)(2,1)S(1)}, u32[]{:S(2)}) copy-start(bf16[256,384]{1,0:T(8,128)(2,1)S(1)} %get-tuple-element.29.m_lo) | copy-start | bytes 589828
  11.2 18.5 %copy-start.5 = (bf16[256,384]{1,0:T(8,128)(2,1)}, bf16[256,384]{1,0:T(8,128)(2,1)S(1)}, u32[]{:S(2)}) copy-start(bf16[256,384]{1,0:T(8,128)(2,1)S(1)} %get-tuple-element.30.m_hi) | copy-start | bytes 589828
  28.0 22.3 %copy-start = (f32[1536,384]{1,0:T(8,128)}, f32[1536,384]{1,0:T(8,128)S(1)}, u32[]{:S(2)}) copy-start(f32[1536,384]{1,0:T(8,128)S(1)} %forward_one.1) | copy-start | bytes 7077892
  29.2 28.1 %collective-permute-start = (f32[768,384]{1,0:T(8,128)}, f32[768,384]{1,0:T(8,128)}, u32[]{:S(2)}, u32[]{:S(2)}) collective-permute-start(f32[768,384]{1,0:T(8,128)} %slice.73), channel_id=1, source_target_pairs={{0,1},{1,0},{2,3},{3,2},{4,5},{5,4},{6,7},{7,6},{8,9},{9,8},{10,11... | collective-permute-start | bytes 3538952 | tf_op jit(solution)/shard_map/ppermute | solution.py:371
  51.5 38.2 %collective-permute-start.8 = (f32[768,384]{1,0:T(8,128)}, f32[768,384]{1,0:T(8,128)}, u32[]{:S(2)}, u32[]{:S(2)}) collective-permute-start(f32[768,384]{1,0:T(8,128)} %slice.65), channel_id=1, source_target_pairs={{0,1},{1,0},{2,3},{3,2},{4,5},{5,4},{6,7},{7,6},{8,9},{9,8},{10,11... | collective-permute-start | bytes 3538952 | tf_op jit(solution)/shard_map/ppermute | solution.py:371
  53.6 3.7 %copy-start.1 = (f32[1536,384]{1,0:T(8,128)S(1)}, f32[1536,384]{1,0:T(8,128)}, u32[]{:S(2)}) copy-start(f32[1536,384]{1,0:T(8,128)} %copy-done) | copy-start | bytes 7077892
  55.6 64.2 %collective-permute-start.12 = (f32[16,16]{1,0:T(8,128)S(1)}, f32[16,16]{1,0:T(8,128)S(1)}, u32[]{:S(2)}, u32[]{:S(2)}) collective-permute-start(f32[16,16]{1,0:T(8,128)S(1)} %select_reduce_fusion), channel_id=1, source_target_pairs={{0,1},{1,0},{2,3},{3,2},{4,5},{5,4},{6,7},{7,6},{8,9},{9,8},{10,11... | collective-permute-start | bytes 3080 | tf_op jit(solution)/shard_map/ppermute | solution.py:373
  58.7 16.6 %collective-permute-start.1 = (f32[384,384]{1,0:T(8,128)S(1)}, f32[384,384]{1,0:T(8,128)S(1)}, u32[]{:S(2)}, u32[]{:S(2)}) collective-permute-start(f32[384,384]{1,0:T(8,128)S(1)} %slice.75), channel_id=1, source_target_pairs={{0,2},{1,3},{2,0},{3,1},{4,6},{5,7},{6,4},{7,5},{8,10},{9,11},{10,... | collective-permute-start | bytes 1769480 | tf_op jit(solution)/shard_map/ppermute | solution.py:371
  75.4 0.8 copy-start.13
  77.0 9.1 %collective-permute-start.2 = (f32[192,384]{1,0:T(8,128)}, f32[192,384]{1,0:T(8,128)}, u32[]{:S(2)}, u32[]{:S(2)}) collective-permute-start(f32[192,384]{1,0:T(8,128)} %slice.77), channel_id=1, source_target_pairs={{0,4},{1,5},{2,6},{3,7},{4,0},{5,1},{6,2},{7,3},{8,12},{9,13},{10,... | collective-permute-start | bytes 884744 | tf_op jit(solution)/shard_map/ppermute | solution.py:371
  78.8 7.2 %copy-start.14 = (f32[384,384]{1,0:T(8,128)S(1)}, f32[384,384]{1,0:T(8,128)}, u32[]{:S(2)}) copy-start(f32[384,384]{1,0:T(8,128)} %copy-done.13) | copy-start | bytes 1769476
  87.1 8.9 %copy-start.2 = (bf16[8,256,128]{2,1,0:T(8,128)(2,1)S(1)}, bf16[8,256,128]{2,1,0:T(8,128)(2,1)}, u32[]{:S(2)}) copy-start(bf16[8,256,128]{2,1,0:T(8,128)(2,1)} %and_convert_fusion.gather) | copy-start | bytes 1572868
  87.1 8.9 %collective-permute-start.3 = (f32[96,384]{1,0:T(8,128)S(1)}, f32[96,384]{1,0:T(8,128)S(1)}, u32[]{:S(2)}, u32[]{:S(2)}) collective-permute-start(f32[96,384]{1,0:T(8,128)S(1)} %slice.79), channel_id=1, source_target_pairs={{0,8},{1,9},{2,10},{3,11},{4,12},{5,13},{6,14},{7,15},{8,0},{9,1},... | collective-permute-start | bytes 442376 | tf_op jit(solution)/shard_map/ppermute | solution.py:371
  91.1 7.6 %copy-start.16 = (bf16[16,16]{1,0:T(8,128)(2,1)S(1)}, bf16[16,16]{1,0:T(8,128)(2,1)}, u32[]{:S(2)}) copy-start(bf16[16,16]{1,0:T(8,128)(2,1)} %param.12) | copy-start | bytes 1540
  91.2 17.9 %collective-permute-start.9 = (f32[384,384]{1,0:T(8,128)S(1)}, f32[384,384]{1,0:T(8,128)S(1)}, u32[]{:S(2)}, u32[]{:S(2)}) collective-permute-start(f32[384,384]{1,0:T(8,128)S(1)} %slice.83), channel_id=1, source_target_pairs={{0,2},{1,3},{2,0},{3,1},{4,6},{5,7},{6,4},{7,5},{8,10},{9,11},{10,... | collective-permute-start | bytes 1769480 | tf_op jit(solution)/shard_map/ppermute | solution.py:371
  98.7 9.2 %collective-permute-start.4 = (f32[96,384]{1,0:T(8,128)S(1)}, f32[96,384]{1,0:T(8,128)S(1)}, u32[]{:S(2)}, u32[]{:S(2)}) collective-permute-start(f32[96,384]{1,0:T(8,128)S(1)} %mix.1), channel_id=1, source_target_pairs={{0,8},{1,9},{2,10},{3,11},{4,12},{5,13},{6,14},{7,15},{8,0},{9,1},... | collective-permute-start | bytes 442376 | tf_op jit(solution)/shard_map/ppermute | solution.py:379
  107.9 10.9 %copy-start.10 = (f32[96,384]{1,0:T(8,128)}, f32[96,384]{1,0:T(8,128)S(1)}, u32[]{:S(2)}) copy-start(f32[96,384]{1,0:T(8,128)S(1)} %collective-permute-done.4) | copy-start | bytes 442372
  107.9 11.7 %copy-start.15 = (pred[8,128,256]{2,1,0:T(8,128)(4,1)S(1)}, pred[8,128,256]{2,1,0:T(8,128)(4,1)}, u32[]{:S(2)}) copy-start(pred[8,128,256]{2,1,0:T(8,128)(4,1)} %get-tuple-element.39) | copy-start | bytes 786436
  107.9 9.9 %collective-permute-start.5 = (f32[192,384]{1,0:T(8,128)S(1)}, f32[192,384]{1,0:T(8,128)S(1)}, u32[]{:S(2)}, u32[]{:S(2)}) collective-permute-start(f32[192,384]{1,0:T(8,128)S(1)} %pad_maximum_fusion.3), channel_id=1, source_target_pairs={{0,4},{1,5},{2,6},{3,7},{4,0},{5,1},{6,2},{7,3},{8,12},{9,13},{10,... | collective-permute-start | bytes 884744 | tf_op jit(solution)/shard_map/ppermute | solution.py:379
  109.1 10.5 %copy-start.12 = (f32[384,384]{1,0:T(8,128)}, f32[384,384]{1,0:T(8,128)S(1)}, u32[]{:S(2)}) copy-start(f32[384,384]{1,0:T(8,128)S(1)} %slice_add_fusion.2) | copy-start | bytes 1769476
  109.9 26.8 %collective-permute-start.10 = (f32[192,384]{1,0:T(8,128)}, f32[192,384]{1,0:T(8,128)}, u32[]{:S(2)}, u32[]{:S(2)}) collective-permute-start(f32[192,384]{1,0:T(8,128)} %slice.85), channel_id=1, source_target_pairs={{0,4},{1,5},{2,6},{3,7},{4,0},{5,1},{6,2},{7,3},{8,12},{9,13},{10,... | collective-permute-start | bytes 884744 | tf_op jit(solution)/shard_map/ppermute | solution.py:371
  117.9 3.5 %copy-start.8 = (f32[192,384]{1,0:T(8,128)}, f32[192,384]{1,0:T(8,128)S(1)}, u32[]{:S(2)}) copy-start(f32[192,384]{1,0:T(8,128)S(1)} %collective-permute-done.5) | copy-start | bytes 884740
  118.8 20.5 %collective-permute-start.6 = (f32[384,384]{1,0:T(8,128)}, f32[384,384]{1,0:T(8,128)}, u32[]{:S(2)}, u32[]{:S(2)}) collective-permute-start(f32[384,384]{1,0:T(8,128)} %pad_maximum_fusion.2), channel_id=1, source_target_pairs={{0,2},{1,3},{2,0},{3,1},{4,6},{5,7},{6,4},{7,5},{8,10},{9,11},{10,... | collective-permute-start | bytes 1769480 | tf_op jit(solution)/shard_map/ppermute | solution.py:379
  119.9 11.6 %collective-permute-start.13 = (f32[16,16]{1,0:T(8,128)S(1)}, f32[16,16]{1,0:T(8,128)S(1)}, u32[]{:S(2)}, u32[]{:S(2)}) collective-permute-start(f32[16,16]{1,0:T(8,128)S(1)} %add.194), channel_id=1, source_target_pairs={{0,2},{1,3},{2,0},{3,1},{4,6},{5,7},{6,4},{7,5},{8,10},{9,11},{10,... | collective-permute-start | bytes 3080 | tf_op jit(solution)/shard_map/ppermute | solution.py:373
  131.5 3.7 %collective-permute-start.14 = (f32[16,16]{1,0:T(8,128)S(1)}, f32[16,16]{1,0:T(8,128)S(1)}, u32[]{:S(2)}, u32[]{:S(2)}) collective-permute-start(f32[16,16]{1,0:T(8,128)S(1)} %add.195), channel_id=1, source_target_pairs={{0,4},{1,5},{2,6},{3,7},{4,0},{5,1},{6,2},{7,3},{8,12},{9,13},{10,... | collective-permute-start | bytes 3080 | tf_op jit(solution)/shard_map/ppermute | solution.py:373
  135.2 5.4 %collective-permute-start.15 = (f32[16,16]{1,0:T(8,128)S(1)}, f32[16,16]{1,0:T(8,128)S(1)}, u32[]{:S(2)}, u32[]{:S(2)}) collective-permute-start(f32[16,16]{1,0:T(8,128)S(1)} %add.196), channel_id=1, source_target_pairs={{0,8},{1,9},{2,10},{3,11},{4,12},{5,13},{6,14},{7,15},{8,0},{9,1},... | collective-permute-start | bytes 3080 | tf_op jit(solution)/shard_map/ppermute | solution.py:373
  137.8 7.7 %collective-permute-start.11 = (f32[96,384]{1,0:T(8,128)S(1)}, f32[96,384]{1,0:T(8,128)S(1)}, u32[]{:S(2)}, u32[]{:S(2)}) collective-permute-start(f32[96,384]{1,0:T(8,128)S(1)} %slice.87), channel_id=1, source_target_pairs={{0,8},{1,9},{2,10},{3,11},{4,12},{5,13},{6,14},{7,15},{8,0},{9,1},... | collective-permute-start | bytes 442376 | tf_op jit(solution)/shard_map/ppermute | solution.py:371
  140.5 13.4 %collective-permute-start.7 = (f32[768,384]{1,0:T(8,128)S(1)}, f32[768,384]{1,0:T(8,128)S(1)}, u32[]{:S(2)}, u32[]{:S(2)}) collective-permute-start(f32[768,384]{1,0:T(8,128)S(1)} %pad_maximum_fusion.1), channel_id=1, source_target_pairs={{0,1},{1,0},{2,3},{3,2},{4,5},{5,4},{6,7},{7,6},{8,9},{9,8},{10,11... | collective-permute-start | bytes 3538952 | tf_op jit(solution)/shard_map/ppermute | solution.py:379
  149.1 3.5 %copy-start.11 = (f32[96,384]{1,0:T(8,128)S(1)}, f32[96,384]{1,0:T(8,128)}, u32[]{:S(2)}) copy-start(f32[96,384]{1,0:T(8,128)} %copy-done.10) | copy-start | bytes 442372
  149.2 3.5 %copy-start.9 = (f32[192,384]{1,0:T(8,128)S(1)}, f32[192,384]{1,0:T(8,128)}, u32[]{:S(2)}) copy-start(f32[192,384]{1,0:T(8,128)} %copy-done.8) | copy-start | bytes 884740
  152.7 1.4 copy-start.4
  152.7 1.4 copy-start.6
  152.7 1.4 copy-start.7
